TPU v7x, 256 devices: a whole 4x4x8 slice. The times are simulated.
256 devices in a mesh: prow: 16 (over z, core), pcol: 16 (over y, x).
Axes of the slice: x: 4, y: 4, z: 8, core: 2. Of those that a mesh axis runs over, the one named last changes fastest.
Arguments:
- root_inverse: float32 [2, 16, 128, 2, 16, 128], P(None, 'prow', None, None, 'pcol'), as said below
- lower_one: float32 [2, 16, 128, 1, 16, 128], P(None, 'prow', None, None, 'pcol'), may hold values from -0.125 to 0.125
- lower_two: float32 [3, 16, 128, 1, 16, 128], P(None, 'prow', None, None, 'pcol'), may hold values from -0.15625 to 0.15625
- dinv_one: float32 [1, 16, 128, 1, 16, 128], P(None, 'prow', None, None, 'pcol'), as said below
- dinv_two: float32 [1, 16, 128, 1, 16, 128], P(None, 'prow', None, None, 'pcol'), as said below
- seg_one: int32 [16], replicated, may hold values from 0 to 2, as said below
- seg_two: int32 [16], replicated, may hold values from 0 to 3, as said below
- parent_two: int32 [4], replicated, may hold values from 0 to 2
- pattern_one: int32 [3, 32], replicated, may hold values 0 or 1
- pattern_two: int32 [4, 48], replicated, may hold values 0 or 1
Outputs:
- inverse_one: float32 [1, 16, 128, 1, 16, 128], P(None, 'prow', None, None, 'pcol')
- inverse_two: float32 [1, 16, 128, 1, 16, 128], P(None, 'prow', None, None, 'pcol')
Inputs may be any that keep to these rules, and one draw needn't show every extreme that they name: `root_inverse`: Block-diagonal over supernodes is not implied; this is a symmetric matrix. `dinv_one`: Symmetric, and zero in every block whose row and column blocks belong to different supernodes of seg_one. `dinv_two`: Symmetric, and zero in every block whose row and column blocks belong to different supernodes of seg_two. `seg_one`: never falls; every supernode 0 to 2 has 1 to 8 consecutive blocks, one exactly 8. `seg_two`: never falls; every supernode 0 to 3 has 1 to 8 consecutive blocks, one exactly 8.
All inputs are finite; a program needn't handle non-finite values.
Results may differ from a plain program's by a relative error of at most 0.00005.
Values sent between devices are 32-bit elements; how exact they have to be, the bound alone decides.
A program may use at most 64 MiB of HBM per device.

v0:
```python
import jax
import jax.numpy as jnp
from jax import lax
from jax.sharding import PartitionSpec as P

highest = lax.Precision.HIGHEST


def contract(left_side, right_side):
    return lax.dot_general(
        left_side,
        right_side,
        (((0,), (0,)), ((), ())),
        precision=highest,
        preferred_element_type=jnp.float32,
    )


def flatten_local(blocks):
    squeezed = blocks[:, 0, :, :, 0, :]
    return squeezed.reshape(
        squeezed.shape[0] * squeezed.shape[1], squeezed.shape[2] * squeezed.shape[3]
    )


def to_blocks(matrix, block_width):
    return matrix.reshape(
        matrix.shape[0] // block_width,
        1,
        block_width,
        matrix.shape[1] // block_width,
        1,
        block_width,
    )


def apply_mask(matrix, block_mask, block_width):
    row_blocks = block_mask.shape[0]
    col_blocks = block_mask.shape[1]
    shaped = matrix.reshape(row_blocks, block_width, col_blocks, block_width)
    return (shaped * block_mask[:, None, :, None]).reshape(
        row_blocks * block_width, col_blocks * block_width
    )


def split_rows(matrix, pieces, block_width):
    return matrix.reshape(
        matrix.shape[0] // (pieces * block_width), pieces, block_width, matrix.shape[1]
    )


def merge_rows(blocks):
    return blocks.reshape(blocks.shape[0] * blocks.shape[1] * blocks.shape[2], blocks.shape[3])


def row_panel(gathered):
    picked = gathered[:, 0]
    return picked.reshape(
        picked.shape[0] * picked.shape[1], picked.shape[2] * picked.shape[3] * picked.shape[4]
    )


def same_mask(first_ids, second_ids):
    return (first_ids[:, None] == second_ids[None, :]).astype(jnp.float32)


def on_device(
    root_inverse,
    lower_one,
    lower_two,
    dinv_one,
    dinv_two,
    seg_one,
    seg_two,
    parent_two,
    pattern_one,
    pattern_two,
):
    block_width = root_inverse.shape[2]
    prow_total = lax.axis_size("prow")
    pcol_total = lax.axis_size("pcol")
    prow_place = lax.axis_index("prow")
    pcol_place = lax.axis_index("pcol")
    root_blocks = pattern_one.shape[1]
    first_nodes = pattern_one.shape[0]
    second_nodes = pattern_two.shape[0]

    def row_ids(amount):
        return jnp.arange(amount, dtype=jnp.int32) * prow_total + prow_place

    def col_ids(amount):
        return jnp.arange(amount, dtype=jnp.int32) * pcol_total + pcol_place

    root_rows = row_ids(root_inverse.shape[0])
    first_cols = col_ids(lower_one.shape[3])
    seg_cols = seg_one[first_cols]
    pick_first = same_mask(seg_cols, jnp.arange(first_nodes, dtype=jnp.int32))
    mask_one = jnp.dot(pick_first, pattern_one[:, root_rows].astype(jnp.float32)).T
    masked_one = apply_mask(flatten_local(lower_one), mask_one, block_width)
    second_rows = row_ids(lower_two.shape[0])
    second_cols = col_ids(lower_two.shape[3])
    seg_two_cols = seg_two[second_cols]
    parent_cols = parent_two[seg_two_cols]
    pick_second = same_mask(seg_two_cols, jnp.arange(second_nodes, dtype=jnp.int32))
    own_pattern = jnp.dot(pick_second, pattern_two[:, second_rows].astype(jnp.float32))
    pick_parent = same_mask(parent_cols, jnp.arange(first_nodes, dtype=jnp.int32))
    root_reach = jnp.dot(
        pick_parent, pattern_one[:, jnp.minimum(second_rows, root_blocks - 1)].astype(jnp.float32)
    )
    level_index = jnp.clip(second_rows - root_blocks, 0, seg_one.shape[0] - 1)
    level_reach = (seg_one[level_index][None, :] == parent_cols[:, None]).astype(jnp.float32)
    reachable = jnp.where((second_rows < root_blocks)[None, :], root_reach, level_reach)
    mask_two = (own_pattern * reachable).T
    masked_two = apply_mask(flatten_local(lower_two), mask_two, block_width)
    root_local = flatten_local(root_inverse)
    root_gathered, first_gathered, second_gathered = (
        lax.all_gather(root_inverse, "pcol", axis=4, tiled=True),
        lax.all_gather(to_blocks(masked_one, block_width), "pcol", axis=4, tiled=True),
        lax.all_gather(to_blocks(masked_two, block_width), "pcol", axis=4, tiled=True),
    )
    root_full = row_panel(root_gathered)
    first_full = row_panel(first_gathered)
    second_full = row_panel(second_gathered)
    turned_part = split_rows(contract(first_full, root_local), prow_total, block_width)
    solved_part = split_rows(contract(root_full, masked_one), prow_total, block_width)
    solved_blocks, turned_blocks = (
        lax.psum_scatter(solved_part, "prow", scatter_dimension=1, tiled=True),
        lax.psum_scatter(turned_part, "prow", scatter_dimension=1, tiled=True),
    )
    solved_one = merge_rows(solved_blocks)
    turned_one = merge_rows(turned_blocks)
    diag_part = split_rows(contract(first_full, solved_one), prow_total, block_width)
    diag_one = merge_rows(lax.psum_scatter(diag_part, "prow", scatter_dimension=1, tiled=True))
    same_one = same_mask(seg_one[row_ids(dinv_one.shape[0])], seg_one[col_ids(dinv_one.shape[3])])
    inverse_one = apply_mask(flatten_local(dinv_one) + diag_one, same_one, block_width)
    region = jnp.concatenate(
        [
            jnp.concatenate([root_local, -solved_one], axis=1),
            jnp.concatenate([-turned_one, inverse_one], axis=1),
        ],
        axis=0,
    )
    region_gathered = lax.all_gather(to_blocks(region, block_width), "pcol", axis=4, tiled=True)
    product_part = split_rows(
        contract(row_panel(region_gathered), masked_two), prow_total, block_width
    )
    solved_two = merge_rows(lax.psum_scatter(product_part, "prow", scatter_dimension=1, tiled=True))
    diag_two_part = split_rows(contract(second_full, solved_two), prow_total, block_width)
    diag_two = merge_rows(lax.psum_scatter(diag_two_part, "prow", scatter_dimension=1, tiled=True))
    same_two = same_mask(seg_two[row_ids(dinv_two.shape[0])], seg_two[col_ids(dinv_two.shape[3])])
    inverse_two = apply_mask(flatten_local(dinv_two) + diag_two, same_two, block_width)
    return (to_blocks(inverse_one, block_width), to_blocks(inverse_two, block_width))


def solution(mesh):
    return jax.shard_map(
        on_device,
        mesh=mesh,
        in_specs=(
            P(None, "prow", None, None, "pcol", None),
            P(None, "prow", None, None, "pcol", None),
            P(None, "prow", None, None, "pcol", None),
            P(None, "prow", None, None, "pcol", None),
            P(None, "prow", None, None, "pcol", None),
            P(),
            P(),
            P(),
            P(),
            P(),
        ),
        out_specs=(
            P(None, "prow", None, None, "pcol", None),
            P(None, "prow", None, None, "pcol", None),
        ),
        check_vma=False,
    )
```

profile of v0, /device:TPU:1, one launch (start us, length us, event | category | flops | bytes accessed | tf_op | source)
XLA Modules:
  0.0 627.4 jit_solution(16628335298792741638)
XLA Ops:
  14.1 56.7 %all-gather.7.cloned.1.call-done = f32[2,1,128,2,16,128]{5,2,3,1,0,4:T(8,128)} async-done(((f32[2,1,128,2,1,128]{5,2,3,1,0,4:T(8,128)}), f32[2,1,128,2,16,128]{5,2,3,1,0,4:T(8,128)}) %all-gather.7.cloned.1.call-update) | async-done | bytes 4194320 | tf_op jit(solution)/shard_map/all_gather | solution.py:117
  70.8 6.6 %copy.54 = f32[2,1,128,2,16,128]{5,4,3,2,0,1:T(8,128)} copy(f32[2,1,128,2,16,128]{5,2,3,1,0,4:T(8,128)} %all-gather.7.cloned.1.call-done) | data formatting | bytes 8388608 | tf_op jit(solution)/shard_map/all_gather | solution.py:117
  77.5 5.0 reshape_squeeze.20
  82.4 4.5 convolution_bitcast_fusion.1
  89.5 32.6 %all-gather.5.cloned.1.call-done = f32[2,1,128,1,16,128]{5,2,3,1,0,4:T(8,128)} async-done(((f32[2,1,128,1,1,128]{5,2,3,1,0,4:T(8,128)}), f32[2,1,128,1,16,128]{5,2,3,1,0,4:T(8,128)}) %all-gather.5.cloned.1.call-update) | async-done | bytes 2097168 | tf_op jit(solution)/shard_map/all_gather | solution.py:118
  122.1 2.8 copy.51
  124.9 2.2 copy.79
  129.0 3.1 convolution_bitcast_fusion
  132.4 48.9 %reduce-scatter.8.cloned.1.call-done = f32[2,1,128,128]{3,2,0,1:T(8,128)} async-done(((f32[2,16,128,128]{3,2,0,1:T(8,128)}), f32[2,1,128,128]{3,2,0,1:T(8,128)}) %reduce-scatter.8.cloned.1.call-update) | async-done | bytes 131088 | tf_op jit(solution)/shard_map/reduce_scatter | solution.py:127
  181.3 3.8 convolution_bitcast_fusion.2
  186.4 54.9 %reduce-scatter.12.cloned.1.call-done = f32[1,1,128,256]{3,2,1,0:T(8,128)} async-done(((f32[1,16,128,256]{3,2,1,0:T(8,128)}), f32[1,1,128,256]{3,2,1,0:T(8,128)}) %reduce-scatter.12.cloned.1.call-update) | async-done | bytes 131088 | tf_op jit(solution)/shard_map/reduce_scatter | solution.py:128
  242.3 57.2 %reduce-scatter.10.cloned.1.call-done = f32[1,1,128,128]{3,2,1,0:T(8,128)} async-done(((f32[1,16,128,128]{3,2,1,0:T(8,128)}), f32[1,1,128,128]{3,2,1,0:T(8,128)}) %reduce-scatter.10.cloned.1.call-update) | async-done | bytes 65552 | tf_op jit(solution)/shard_map/reduce_scatter | solution.py:133
  308.2 75.8 %all-gather.11.cloned.1.call-done = f32[3,1,128,3,16,128]{5,2,3,1,0,4:T(8,128)} async-done(((f32[3,1,128,3,1,128]{5,2,3,1,0,4:T(8,128)}), f32[3,1,128,3,16,128]{5,2,3,1,0,4:T(8,128)}) %all-gather.11.cloned.1.call-update) | async-done | bytes 9437200 | tf_op jit(solution)/shard_map/all_gather | solution.py:143
  384.0 12.8 %copy.63 = f32[3,1,128,3,16,128]{5,4,3,2,0,1:T(8,128)} copy(f32[3,1,128,3,16,128]{5,2,3,1,0,4:T(8,128)} %all-gather.11.cloned.1.call-done) | data formatting | bytes 18874368 | tf_op jit(solution)/shard_map/all_gather | solution.py:143
  396.8 10.0 %reshape_squeeze.24 = f32[384,6144]{1,0:T(8,128)} reshape(f32[3,1,128,3,16,128]{5,4,3,2,0,1:T(8,128)} %copy.63) | data formatting | bytes 18874368 | tf_op jit(solution)/shard_map/reshape;squeeze | solution.py:58
  406.8 9.6 %copy.64 = f32[6144,384]{1,0:T(8,128)} copy(f32[6144,384]{0,1:T(8,128)} %bitcast.148) | data formatting | bytes 18874368 | tf_op jit(solution)/shard_map/dot_general | solution.py:10
  416.4 11.0 %fusion.25 = f32[3,16,128,128]{3,2,1,0:T(8,128)} fusion(f32[3,16,128,384]{3,2,1,0:T(8,128)} %bitcast.149, f32[384,128,1,1]{1,0,3,2:T(8,128)S(1)} %bitcast.160), kind=kOutput, calls=%fused_computation.60 | convolution fusion | flops 3623878656 | bytes 12779520 | tf_op jit(solution)/shard_map/dot_general | solution.py:10
  428.7 10.5 %all-gather.9.cloned.1.call-done = f32[3,1,128,1,16,128]{5,2,3,1,0,4:T(8,128)} async-done(((f32[3,1,128,1,1,128]{5,2,3,1,0,4:T(8,128)}), f32[3,1,128,1,16,128]{5,2,3,1,0,4:T(8,128)}) %all-gather.9.cloned.1.call-update) | async-done | bytes 3145744 | tf_op jit(solution)/shard_map/all_gather | solution.py:119
  439.2 3.7 copy.60
  442.9 3.1 copy.78
  446.0 2.4 copy.61
  448.4 110.4 %all-reduce.3.cloned.1.call-done = f32[3,16,128,128]{3,2,1,0:T(8,128)} async-done(((f32[3,16,128,128]{3,2,1,0:T(8,128)}), f32[3,16,128,128]{3,2,1,0:T(8,128)}) %all-reduce.3.cloned.1.call-update) | async-done | bytes 3145744
  560.4 3.7 convolution_bitcast_fusion.3
  566.0 53.4 %reduce-scatter.14.cloned.1.call-done = f32[1,1,128,128]{3,2,1,0:T(8,128)} async-done(((f32[1,16,128,128]{3,2,1,0:T(8,128)}), f32[1,1,128,128]{3,2,1,0:T(8,128)}) %reduce-scatter.14.cloned.1.call-update) | async-done | bytes 65552 | tf_op jit(solution)/shard_map/reduce_scatter | solution.py:149
  (78 shorter events, 24.5 us)
Async XLA Ops:
  7.2 63.6 %all-gather.7.cloned.1.call-start = ((), (), s32[]{:S(2)}) async-start(), calls=%async_computation.5 | async-start | bytes 4456448 | tf_op jit(solution)/shard_map/all_gather | solution.py:117
  8.9 113.2 %all-gather.5.cloned.1.call-start = ((), (), s32[]{:S(2)}) async-start(), calls=%async_computation.4 | async-start | bytes 2228224 | tf_op jit(solution)/shard_map/all_gather | solution.py:118
  14.1 167.2 %reduce-scatter.8.cloned.1.call-start = ((), (), s32[]{:S(2)}) async-start(), calls=%async_computation.6 | async-start | bytes 2228224 | tf_op jit(solution)/shard_map/reduce_scatter | solution.py:127
  77.5 5.0 copy-start.3
  87.3 2.0 copy-start.1
  89.2 152.1 %reduce-scatter.12.cloned.1.call-start = ((), (), s32[]{:S(2)}) async-start(), calls=%async_computation.9 | async-start | bytes 2228224 | tf_op jit(solution)/shard_map/reduce_scatter | solution.py:128
  132.2 167.3 %copy-start.5 = (f32[1,1,128,1,1,128]{5,4,3,2,1,0:T(1,128)S(1)}, f32[1,1,128,1,1,128]{5,4,3,2,1,0:T(1,128)}, u32[]{:S(2)}) copy-start(f32[1,1,128,1,1,128]{5,4,3,2,1,0:T(1,128)} %param.13) | copy-start | bytes 196612
  132.2 167.3 %reduce-scatter.10.cloned.1.call-start = ((), (), s32[]{:S(2)}) async-start(), calls=%async_computation.7 | async-start | bytes 1114112 | tf_op jit(solution)/shard_map/reduce_scatter | solution.py:133
  181.3 61.0 %copy-start.4 = (f32[2,1,128,128]{3,2,0,1:T(8,128)S(1)}, f32[2,1,128,128]{3,2,0,1:T(8,128)}, u32[]{:S(2)}) copy-start(f32[2,1,128,128]{3,2,0,1:T(8,128)} %reduce-scatter.8.cloned.1.call-done) | copy-start | bytes 393220
  185.1 118.3 %copy-start = (s32[16]{0:T(128)S(1)}, s32[16]{0:T(128)}, u32[]{:S(2)}) copy-start(s32[16]{0:T(128)} %param.15) | copy-start | bytes 196
  185.1 198.9 %all-gather.11.cloned.1.call-start = ((), (), s32[]{:S(2)}) async-start(), calls=%async_computation.10 | async-start | bytes 10027008 | tf_op jit(solution)/shard_map/all_gather | solution.py:143
  186.4 117.6 %copy-start.9 = (s32[4,48]{1,0:T(4,128)S(1)}, s32[4,48]{1,0:T(4,128)}, u32[]{:S(2)}) copy-start(s32[4,48]{1,0:T(4,128)} %param.19) | copy-start | bytes 2308
  186.4 118.3 %copy-start.10 = (s32[4]{0:T(128)S(1)}, s32[4]{0:T(128)}, u32[]{:S(2)}) copy-start(s32[4]{0:T(128)} %param.17) | copy-start | bytes 52
  186.4 121.0 %copy-start.7 = (f32[3,1,128,1,1,128]{5,4,3,2,1,0:T(1,128)S(1)}, f32[3,1,128,1,1,128]{5,4,3,2,1,0:T(1,128)}, u32[]{:S(2)}) copy-start(f32[3,1,128,1,1,128]{5,4,3,2,1,0:T(1,128)} %param.12) | copy-start | bytes 589828
  301.5 137.6 %all-gather.9.cloned.1.call-start = ((), (), s32[]{:S(2)}) async-start(), calls=%async_computation.8 | async-start | bytes 3342336 | tf_op jit(solution)/shard_map/all_gather | solution.py:119
  308.2 250.7 %all-reduce.3.cloned.1.call-start = ((), (), s32[]{:S(2)}) async-start(), calls=%async_computation.12 | async-start | bytes 6291456
  406.8 9.6 %copy-start.2 = (f32[3,1,128,1,1,128]{5,2,3,1,0,4:T(8,128)S(1)}, f32[3,1,128,1,1,128]{5,2,3,1,0,4:T(8,128)}, u32[]{:S(2)}) copy-start(f32[3,1,128,1,1,128]{5,2,3,1,0,4:T(8,128)} %broadcast_multiply_fusion) | copy-start | bytes 589828
  427.4 0.7 copy-start.11
  427.5 191.9 %reduce-scatter.14.cloned.1.call-start = ((), (), s32[]{:S(2)}) async-start(), calls=%async_computation.11 | async-start | bytes 1114112 | tf_op jit(solution)/shard_map/reduce_scatter | solution.py:149
  448.4 116.9 %copy-start.6 = (f32[1,1,128,128]{3,2,1,0:T(8,128)S(1)}, f32[1,1,128,128]{3,2,1,0:T(8,128)}, u32[]{:S(2)}) copy-start(f32[1,1,128,128]{3,2,1,0:T(8,128)} %reduce-scatter.10.cloned.1.call-done) | copy-start | bytes 196612
  448.4 170.9 %copy-start.8 = (f32[1,1,128,1,1,128]{5,4,3,2,1,0:T(1,128)S(1)}, f32[1,1,128,1,1,128]{5,4,3,2,1,0:T(1,128)}, u32[]{:S(2)}) copy-start(f32[1,1,128,1,1,128]{5,4,3,2,1,0:T(1,128)} %param.14) | copy-start | bytes 196612
Sparse Core Ops, SparseCore 0:
  10.4 60.3 all-gather.6
  73.2 48.8 all-gather.4
  124.7 56.5 reduce-scatter.7
  183.7 57.6 reduce-scatter.11
  243.7 55.7 reduce-scatter.9
  302.1 81.8 all-gather.10
  386.7 52.3 all-gather.8
  441.7 117.1 all-reduce.2
  564.3 55.0 reduce-scatter.13
where the time goes:
time: 630 us; the launch traced here: 627 us
  waiting for transfers between devices  500 us (79%)
  local copies, waits for them, and re-layouts  73.2 us (12%)
  matrix products  28.3 us (4%)
  between operations  18.2 us (3%)
  other arithmetic  6.39 us (1%)
    unnamed x10, waiting for transfers between devices  111 us
    all_gather x1, waiting for transfers between devices, on_device(): lax.all_gather(to_blocks(region, block_width), 'pcol', axis=4, tiled=True)  75.8 us
    reduce_scatter x1, waiting for transfers between devices, on_device(): lax.psum_scatter(diag_part, 'prow', scatter_dimension=1, tiled=True)  57.2 us
    all_gather x1, waiting for transfers between devices, on_device(): lax.all_gather(root_inverse, 'pcol', axis=4, tiled=True)  56.7 us
    reduce_scatter x1, waiting for transfers between devices, on_device(): lax.psum_scatter(turned_part, 'prow', scatter_dimension=1, tiled=True)  54.9 us
    reduce_scatter x1, waiting for transfers between devices, on_device(): lax.psum_scatter(diag_two_part, 'prow', scatter_dimension=1, tiled=True)  53.4 us
    reduce_scatter x1, waiting for transfers between devices, on_device(): lax.psum_scatter(solved_part, 'prow', scatter_dimension=1, tiled=True)  48.9 us
    all_gather x1, waiting for transfers between devices, on_device(): lax.all_gather(to_blocks(masked_one, block_width), 'pcol', axis=4, tiled=...  32.6 us
  transfers between devices with their start and end apart: 9, of which 9 were waited for; matrix products, arithmetic and copies ran while one was open for 15% of the time, Pallas kernels for 0%

commit v1 on v0

v1 whole, which is shorter than its diff:
```python
import jax
import jax.numpy as jnp
from jax import lax
from jax.experimental import pallas as pl
from jax.experimental.pallas import tpu as pltpu
from jax.sharding import PartitionSpec as P

MESH = pl.DeviceIdType.MESH
F32 = jnp.float32
BF16 = jnp.bfloat16
B = 128
NX = 4
NY = 4
NZ = 8
NB = 16

GATHER = 40
M_G1 = 0
M_GE = M_G1 + GATHER
M_BD = M_GE + GATHER
M_BZ = M_BD + GATHER
M_Y1 = M_BZ + 15
M_Y2 = M_Y1 + 15
M_Z1 = M_Y2 + 15
M_Z2 = M_Z1 + 15
M_T1 = M_Z2 + 15
M_T2 = M_T1 + 2
M_F1 = M_T2 + 2
M_F2 = M_F1 + 1
M_ALL = M_F2 + 1


def split(x):
    hi = x.astype(BF16)
    lo = (x - hi.astype(F32)).astype(BF16)
    return hi, lo


def left3(x):
    hi, lo = split(x)
    return jnp.concatenate([hi, hi, lo], axis=1)


def right3(x):
    hi, lo = split(x)
    return jnp.concatenate([hi, lo, hi], axis=0)


def dot(a, b):
    return jnp.dot(a, b, preferred_element_type=F32)


def rounds(*flows):
    flows = list(flows)
    while flows:
        for flow in list(flows):
            try:
                next(flow)
            except StopIteration:
                flows.remove(flow)


def kernel(
    seg1, seg2, par2, pat1, pat2,
    r_ref, l1_ref, l2_ref, d1_ref, d2_ref,
    o1_ref, o2_ref,
    g1, ge, gbd, bz,
    p1, x1, rp1, rm1,
    p2, x2, rp2, rm2,
    pz1, xz1, rpz1, rmz1,
    pz2, xz2, rpz2, rmz2,
    yt1, yt2, w1, w2, rw, ew,
    send, recv,
):
    p = lax.axis_index("prow")
    q = lax.axis_index("pcol")
    z = p // 2
    c = p % 2
    y = q // NX
    x = q % NX
    sibling = (2 * z + 1 - c, q)
    z_up = (2 * ((z + 1) % NZ) + c, q)
    z_down = (2 * ((z + NZ - 1) % NZ) + c, q)
    diagonal = p == q
    pending = []

    def remote(m, src, dst, device):
        return pltpu.make_async_remote_copy(
            src_ref=src,
            dst_ref=dst,
            send_sem=send.at[m],
            recv_sem=recv.at[m],
            device_id=device,
            device_id_type=MESH,
        )

    def push(m, src, dst, device):
        copy = remote(m, src, dst, device)
        copy.start()
        pending.append(copy)

    def arrive(m, dst):
        remote(m, dst, dst, sibling).wait_recv()

    s1 = seg1[q]
    s2 = seg2[q]
    parent = par2[s2]
    for a in range(2):
        m1 = pat1[s1, p + NB * a].astype(F32)
        g1[a, q] = (l1_ref[pl.ds(B * a, B), :] * m1).T
    mb = (pat2[s2, 2 * NB + p] * (seg1[p] == parent).astype(jnp.int32)).astype(F32)
    own_b = (l2_ref[pl.ds(2 * B, B), :] * mb).T
    bz[p] = own_b
    gbd[0, q] = own_b
    gbd[1, q] = d1_ref[...].T

    barrier = pltpu.get_barrier_semaphore()
    plane = [
        (p, y * NX + (x + 1) % NX),
        (p, y * NX + (x + NX - 1) % NX),
        (p, ((y + 1) % NY) * NX + x),
        (p, ((y + NY - 1) % NY) * NX + x),
    ]
    for device in plane + [sibling, z_up, z_down]:
        pl.semaphore_signal(barrier, inc=1, device_id=device, device_id_type=MESH)
    for i in range(2):
        source = 2 * (q // 2) + i

        @pl.when(jnp.logical_not(diagonal & (c == i)))
        def _():
            pl.semaphore_signal(barrier, inc=1, device_id=(source, p), device_id_type=MESH)

    pl.semaphore_wait(barrier, 9 - diagonal.astype(jnp.int32))

    def gather(g, base):
        top, low, whole = pl.ds(0, B // 2), pl.ds(B // 2, B // 2), pl.ds(0, B)

        class Half:
            pass

        halves = []
        for h in range(2):
            s = Half()
            s.h, s.base = h, base + 20 * h
            s.u, s.v = (x, y) if h == 0 else (y, x)
            halves.append(s)

        def slot(s, du, dv, rows):
            u, v = (s.u + du) % 4, (s.v + dv) % 4
            k = v * NX + u if s.h == 0 else u * NX + v
            return g.at[s.h, k, rows]

        def device(s, du, dv):
            u, v = (s.u + du) % 4, (s.v + dv) % 4
            return (p, v * NX + u if s.h == 0 else u * NX + v)

        def first(s, m, du, step, rows):
            view = slot(s, du, 0, rows)
            push(s.base + m, view, view, device(s, step, 0))

        def second(s, m, du, dv, step, rows):
            view = slot(s, du, dv, rows)
            push(s.base + m, view, view, device(s, 0, step))

        def spread(s, i, du):
            second(s, 4 + 2 * i, du, 0, 1, whole)
            second(s, 5 + 2 * i, du, 0, 3, whole)

        def pass_on(s, i, du):
            arrive(s.base + 4 + 2 * i, slot(s, du, 3, whole))
            second(s, 12 + 2 * i, du, 3, 1, top)
            arrive(s.base + 5 + 2 * i, slot(s, du, 1, whole))
            second(s, 13 + 2 * i, du, 1, 3, low)

        offsets = (0, 3, 1, 2)
        for s in halves:
            first(s, 0, 0, 1, whole)
            first(s, 1, 0, 3, whole)
        for s in halves:
            spread(s, 0, 0)
        yield
        for s in halves:
            arrive(s.base, slot(s, 3, 0, whole))
            first(s, 2, 3, 1, top)
            spread(s, 1, 3)
            arrive(s.base + 1, slot(s, 1, 0, whole))
            first(s, 3, 1, 3, low)
            spread(s, 2, 1)
        yield
        for s in halves:
            pass_on(s, 0, 0)
        yield
        for s in halves:
            arrive(s.base + 2, slot(s, 2, 0, top))
            arrive(s.base + 3, slot(s, 2, 0, low))
            spread(s, 3, 2)
        yield
        for i in (1, 2):
            for s in halves:
                pass_on(s, i, offsets[i])
        yield
        for s in halves:
            pass_on(s, 3, 2)
        yield
        for i in range(4):
            for s in halves:
                arrive(s.base + 12 + 2 * i, slot(s, offsets[i], 2, top))
                arrive(s.base + 13 + 2 * i, slot(s, offsets[i], 2, low))

    def column():
        def slot(dz, core):
            return bz.at[2 * ((z + dz + NZ) % NZ) + core]

        def send_to(m, dz, device):
            view = slot(dz, c)
            push(M_BZ + m, view, view, device)

        send_to(0, 0, z_up)
        send_to(4, 0, z_down)
        send_to(7, 0, sibling)
        yield
        for t in range(1, 5):
            arrive(M_BZ + t - 1, slot(-t, c))
            if t < 4:
                send_to(t, -t, z_up)
            send_to(7 + t, -t, sibling)
            if t < 4:
                arrive(M_BZ + 4 + t - 1, slot(t, c))
                if t < 3:
                    send_to(4 + t, t, z_down)
                send_to(11 + t, t, sibling)
            yield
        arrive(M_BZ + 7, slot(0, 1 - c))
        for t in range(1, 5):
            arrive(M_BZ + 7 + t, slot(-t, 1 - c))
            if t < 4:
                arrive(M_BZ + 11 + t, slot(t, 1 - c))

    def reduce(part, other, up, down, base):
        order = (4, -3, 3, -2, 2, -1, 1, 0)

        def pair(off):
            return pl.ds(2 * ((z + off + NZ) % NZ), 2)

        for n, off in enumerate(order):
            push(base + n, part.at[1 - c, pair(off)], other.at[pair(off)], sibling)
        yield

        def own(n):
            arrive(base + n, other.at[pair(order[n])])
            return part[c, pair(order[n])] + other[pair(order[n])]

        for t in range(4):
            n = 2 * t
            total = own(n)
            if t > 0:
                arrive(base + 8 + t - 1, up.at[t - 1])
                total = total + up[t - 1]
            part[c, pair(order[n])] = total
            push(base + 8 + t, part.at[c, pair(order[n])], up.at[t], z_up)
            if t < 3:
                n = 2 * t + 1
                total = own(n)
                if t > 0:
                    arrive(base + 12 + t - 1, down.at[t - 1])
                    total = total + down[t - 1]
                part[c, pair(order[n])] = total
                push(base + 12 + t, part.at[c, pair(order[n])], down.at[t], z_down)
            yield
        total = own(7)
        arrive(base + 14, down.at[2])
        total = total + down[2]
        arrive(base + 11, up.at[3])
        part[c, pair(0)] = total + up[3]

    def transpose_out(part, yt, base):
        for i in range(2):
            mine = part.at[c, 2 * z + i]
            copy = pltpu.make_async_remote_copy(
                src_ref=mine,
                dst_ref=yt.at[c],
                send_sem=send.at[base + i],
                recv_sem=recv.at[base + c],
                device_id=(q, 2 * z + i),
                device_id_type=MESH,
            )
            itself = diagonal & (c == i)

            @pl.when(itself)
            def _():
                yt[c] = part[c, 2 * z + i]

            @pl.when(jnp.logical_not(itself))
            def _():
                copy.start()

    def transpose_sent(part, yt, base):
        for i in range(2):
            @pl.when(jnp.logical_not(diagonal & (c == i)))
            def _():
                remote(base + i, part.at[c, 2 * z + i], yt.at[c], (q, 2 * z + i)).wait_send()

    def transpose_in(yt, base):
        for i in range(2):
            @pl.when(jnp.logical_not(diagonal & (c == i)))
            def _():
                arrive(base + i, yt.at[i])
        return right3(jnp.concatenate([yt[0].T, yt[1].T], axis=0))

    GROUP = 4

    def panel(g, i):
        rows = pl.ds(i * GROUP, GROUP)
        return jnp.concatenate(
            [g[0, rows].reshape(GROUP * B, B), g[1, rows].reshape(GROUP * B, B)], axis=1
        )

    def times_root(g, part):
        @pl.loop(0, NB // GROUP)
        def _(i):
            out = dot(left3(panel(g, i)), rw[...])
            rows = pl.ds(i * GROUP, GROUP)
            part[0, rows] = out[:, :B].reshape(GROUP, B, B)
            part[1, rows] = out[:, B:].reshape(GROUP, B, B)

    def store_halves(part, i, out):
        rows = pl.ds(i * GROUP, GROUP)
        blocks = out.reshape(GROUP, B, B)
        part[0, rows] = blocks[:, : B // 2]
        part[1, rows] = blocks[:, B // 2 :]

    def finish(part, w, base):
        push(base, part.at[c, 2 * z + 1 - c], w.at[c], sibling)
        w[c] = part[c, p]
        arrive(base, w.at[1 - c])

    rw[...] = right3(
        jnp.concatenate(
            [r_ref[pl.ds(0, 2 * B, stride=2), :], r_ref[pl.ds(1, 2 * B, stride=2), :]], axis=1
        )
    )

    rounds(gather(g1, M_G1), column())

    for a in range(2):
        ma = (pat2[s2, p + NB * a] * pat1[parent, p + NB * a]).astype(F32)
        ew[:, pl.ds(B * a, B)] = (l2_ref[pl.ds(B * a, B), :] * ma).T

    @pl.loop(0, NB)
    def _(k):
        right = right3(jnp.concatenate([g1[0, k], g1[1, k]], axis=1))
        ew[...] -= dot(left3(bz[k]), right)

    ge[0, q] = ew[:, :B]
    ge[1, q] = ew[:, B:]

    def second_level():
        yield from gather(ge, M_GE)
        times_root(ge, p2)
        yield from reduce(p2, x2, rp2, rm2, M_Y2)
        transpose_out(p2, yt2, M_T2)
        yield

    def first_level():
        times_root(g1, p1)
        yield from reduce(p1, x1, rp1, rm1, M_Y1)
        transpose_out(p1, yt1, M_T1)
        yield
        right = transpose_in(yt1, M_T1)

        rhs = right

        @pl.loop(0, NB // GROUP)
        def _(i):
            store_halves(pz1, i, dot(left3(panel(g1, i)), rhs))

        yield from reduce(pz1, xz1, rpz1, rmz1, M_Z1)

    def corner():
        for _ in range(6):
            yield
        yield from gather(gbd, M_BD)

    rounds(second_level(), first_level(), corner())

    def corner_step(k, acc):
        return acc + dot(left3(bz[k]), right3(gbd[1, k]))

    u3 = right3(lax.fori_loop(0, NB, corner_step, jnp.zeros((B, B), F32)).T)
    y3 = transpose_in(yt2, M_T2)

    @pl.loop(0, NB // GROUP)
    def _(i):
        rows = pl.ds(i * GROUP, GROUP)
        out = dot(left3(panel(ge, i)), y3)
        out = out + dot(left3(gbd[0, rows].reshape(GROUP * B, B)), u3)
        store_halves(pz2, i, out)

    rounds(reduce(pz2, xz2, rpz2, rmz2, M_Z2))

    finish(pz1, w1, M_F1)
    finish(pz2, w2, M_F2)
    same1 = (seg1[p] == seg1[q]).astype(F32)
    same2 = (seg2[p] == seg2[q]).astype(F32)
    o1_ref[...] = (d1_ref[...] + w1[...].reshape(B, B)) * same1
    o2_ref[...] = (d2_ref[...] + w2[...].reshape(B, B)) * same2

    for copy in pending:
        copy.wait_send()
    transpose_sent(p1, yt1, M_T1)
    transpose_sent(p2, yt2, M_T2)


def on_device(
    root_inverse, lower_one, lower_two, dinv_one, dinv_two,
    seg_one, seg_two, parent_two, pattern_one, pattern_two,
):
    vmem = pl.BlockSpec(memory_space=pltpu.VMEM)
    smem = pl.BlockSpec(memory_space=pltpu.SMEM)

    def buf(*shape, dtype=F32):
        return pltpu.VMEM(shape, dtype)

    def sums(rows):
        return [
            buf(2, NB, rows, B),
            buf(NB, rows, B),
            buf(4, 2, rows, B),
            buf(3, 2, rows, B),
        ]

    outs = pl.pallas_call(
        kernel,
        out_shape=[jax.ShapeDtypeStruct((B, B), F32)] * 2,
        in_specs=[smem] * 5 + [vmem] * 5,
        out_specs=[vmem] * 2,
        scratch_shapes=[
            buf(2, NB, B, B),
            buf(2, NB, B, B),
            buf(2, NB, B, B),
            buf(NB, B, B),
            *sums(B),
            *sums(B),
            *sums(B // 2),
            *sums(B // 2),
            buf(2, B, B),
            buf(2, B, B),
            buf(2, B // 2, B),
            buf(2, B // 2, B),
            buf(6 * B, 2 * B, dtype=BF16),
            buf(B, 2 * B),
            pltpu.SemaphoreType.DMA((M_ALL,)),
            pltpu.SemaphoreType.DMA((M_ALL,)),
        ],
        compiler_params=pltpu.CompilerParams(
            collective_id=0, has_side_effects=True, vmem_limit_bytes=48 << 20
        ),
    )(
        seg_one, seg_two, parent_two, pattern_one, pattern_two,
        root_inverse.reshape(4 * B, B),
        lower_one.reshape(2 * B, B),
        lower_two.reshape(3 * B, B),
        dinv_one.reshape(B, B),
        dinv_two.reshape(B, B),
    )
    return tuple(out.reshape(1, 1, B, 1, 1, B) for out in outs)


def solution(mesh):
    blocks = P(None, "prow", None, None, "pcol", None)
    return jax.shard_map(
        on_device,
        mesh=mesh,
        in_specs=(blocks,) * 5 + (P(),) * 5,
        out_specs=(blocks,) * 2,
        check_vma=False,
    )
```

time: 630 us -> 132 us (0.21)
  waiting for transfers between devices: 500 us -> 0 us
  Pallas kernels: 0 us -> 124 us
  local copies, waits for them, and re-layouts: 73.2 us -> 6.4 us
  matrix products: 28.3 us -> 0 us
  between operations: 18.2 us -> 0.69 us
  other arithmetic: 6.39 us -> 0 us
    reduce_scatter x4 -> x0, waiting for transfers between devices: 214 us -> none  [the longest x1 57.2 us: on_device(): lax.psum_scatter(diag_part, 'prow', scatter_dimension=1, tiled=True)]
    all_gather x4 -> x0, waiting for transfers between devices: 176 us -> none  [the longest x1 75.8 us: on_device(): lax.all_gather(to_blocks(region, block_width), 'pcol', axis=4, tiled=True)]
    pallas_call x0 -> x1, Pallas kernels: none -> 124 us  [on_device(): pl.pallas_call(kernel, out_shape=[jax.ShapeDtypeStruct((B, B), F32)] * 2,...]
    unnamed x10 -> x0, waiting for transfers between devices: 111 us -> none
    dot_general x8 -> x0, matrix products: 28.3 us -> none  [the longest x5 26.1 us: contract(): lax.dot_general(left_side, right_side, (((0,), (0,)), ((), ())), precisio...]
    all_gather x4 -> x0, local copies, waits for them, and re-layouts: 25.9 us -> none  [the longest x1 12.8 us: on_device(): lax.all_gather(to_blocks(region, block_width), 'pcol', axis=4, tiled=True)]
    another operation x3 -> x0, local copies, waits for them, and re-layouts: 15.2 us -> none  [the longest x2 15 us: row_panel(): picked.reshape(picked.shape[0] * picked.shape[1], picked.shape[2] * picke...]
    dot_general x3 -> x0, local copies, waits for them, and re-layouts: 13.9 us -> none  [contract(): lax.dot_general(left_side, right_side, (((0,), (0,)), ((), ())), precisio...]
  transfers between devices with their start and end apart: 9 -> 0, of which waited for: 9 -> 0; matrix products, arithmetic and copies ran while one was open for 15% -> 0% of each run, Pallas kernels for 0% -> 0%
where the time goes in v1:
time: 132 us; the launch traced here: 131 us
  Pallas kernels  124 us (94%)
  local copies, waits for them, and re-layouts  6.4 us (5%)
    pallas_call x1, Pallas kernels, on_device(): pl.pallas_call(kernel, out_shape=[jax.ShapeDtypeStruct((B, B), F32)] * 2,...  124 us
    unnamed x22, local copies, waits for them, and re-layouts  6.4 us

profile of v1, /device:TPU:1, one launch (start us, length us, event | category | flops | bytes accessed | tf_op | source)
XLA Modules:
  0.0 131.4 jit_solution(327981760075650964)
XLA Ops:
  0.6 0.0 copy-start.6
  0.6 0.0 copy-start.5
  0.7 0.0 copy-start.7
  0.7 0.0 copy-start.8
  0.7 0.0 copy-start.9
  0.7 0.6 copy-done.6
  1.3 0.0 copy-done.5
  1.3 0.0 copy-done.7
  1.3 0.0 copy-done.8
  1.3 0.0 copy-done.9
  1.4 0.0 copy-start
  1.4 0.9 copy-done
  2.3 0.0 copy-start.1
  2.3 0.9 copy-done.1
  3.2 0.0 copy-start.2
  3.2 0.9 copy-done.2
  4.1 0.0 copy-start.3
  4.1 0.8 copy-done.3
  5.0 0.0 copy-start.4
  5.0 0.8 copy-done.4
  5.8 124.3 %shard_map.113 = (f32[128,128]{1,0:T(8,128)S(1)}, f32[128,128]{1,0:T(8,128)S(1)}) custom-call(s32[16]{0:T(128)S(1)} %copy-done.7, s32[16]{0:T(128)S(1)} %copy-done.8, s32[4]{0:T(128)S(1)} %copy-done.9, s32[3,32]{1,0:T(4,128)S(1)} %copy-done.5, s32[4,48]{1,0:T(4,128)S(1)} %copy-done.6, f32[512,128]{1,0:T(8,128)S(1)} %bitcast.11, f32[256,128]{1,0:T(8,128)S(1)} %bitcast.13, ...), custom_call_target="tpu_custom_call" | custom-call | tf_op jit(solution)/shard_map/pallas_call | solution.py:432
  130.1 0.6 copy.16
  130.7 0.6 copy.17
Async XLA Ops:
  0.6 0.7 copy-start.6
  0.6 0.7 copy-start.5
  0.7 0.7 copy-start.7
  0.7 0.7 copy-start.8
  0.7 0.7 copy-start.9
  1.4 0.9 copy-start
  2.3 0.9 copy-start.1
  3.2 0.9 copy-start.2
  4.1 0.8 copy-start.3
  5.0 0.8 copy-start.4

commit v2 on v1

v2 whole, which is shorter than its diff:
```python
import jax
import jax.numpy as jnp
from jax import lax
from jax.experimental import pallas as pl
from jax.experimental.pallas import tpu as pltpu
from jax.sharding import PartitionSpec as P

MESH = pl.DeviceIdType.MESH
F32 = jnp.float32
BF16 = jnp.bfloat16
B = 128
NX = 4
NY = 4
NZ = 8
NB = 16

M_ROOT = 0
M_G1 = M_ROOT + 3
M_GE = M_G1 + 30
M_BD = M_GE + 30
M_BZ = M_BD + 30
M_Y1 = M_BZ + 15
M_Y2 = M_Y1 + 20
M_Z1 = M_Y2 + 20
M_Z2 = M_Z1 + 22
M_T1 = M_Z2 + 22
M_T2 = M_T1 + 4
M_F1 = M_T2 + 4
M_F2 = M_F1 + 1
M_ALL = M_F2 + 1
STEPS = (1, 3, 2)
OFFSETS = (0, 3, 1, 2)


def split(x):
    hi = x.astype(BF16)
    lo = (x - hi.astype(F32)).astype(BF16)
    return hi, lo


def left3(x):
    hi, lo = split(x)
    return jnp.concatenate([hi, hi, lo], axis=1)


def right3(x):
    hi, lo = split(x)
    return jnp.concatenate([hi, lo, hi], axis=0)


def dot(a, b):
    return jnp.dot(a, b, preferred_element_type=F32)


def until(flow, *others):
    others = list(others)
    for _ in flow:
        for other in list(others):
            if next(other, "end") == "end":
                others.remove(other)


def rounds(*flows):
    flows = list(flows)
    while flows:
        for flow in list(flows):
            try:
                next(flow)
            except StopIteration:
                flows.remove(flow)


def kernel(
    seg1, seg2, par2, pat1, pat2,
    r_hbm, l1_hbm, l2_hbm, d1_hbm, d2_hbm,
    o1_ref, o2_ref,
    r_ref, l1_ref, l2_ref, d1_ref, d2_ref,
    gr, g1, ge, gbd, bz,
    p1, x1, ch1,
    p2, x2, ch2,
    pz1, xz1, upz1, dnz1,
    pz2, xz2, upz2, dnz2,
    yt1, yt2, w1, w2, ew,
    send, recv, local,
):
    p = lax.axis_index("prow")
    q = lax.axis_index("pcol")
    z = p // 2
    c = p % 2
    y = q // NX
    x = q % NX
    lands = (z + x // 2) % 2 == 0
    odd = jnp.where(lands, 0, 1)
    sibling = (2 * z + 1 - c, q)
    z_up = (2 * ((z + 1) % NZ) + c, q)
    z_down = (2 * ((z + NZ - 1) % NZ) + c, q)
    pending = []
    drains = []

    def at(dx, dy):
        return (p, ((y + dy) % NY) * NX + (x + dx) % NX)

    barrier = pltpu.get_barrier_semaphore()
    partners = [at(1, 0), at(2, 0), at(3, 0), at(0, 1), at(0, 2), at(0, 3)]
    partners += [sibling, z_up, z_down]
    partners += [(2 * z + 1 - c, y * NX + (x + d) % NX) for d in (1, 2, 3)]
    for device in partners:
        pl.semaphore_signal(barrier, inc=1, device_id=device, device_id_type=MESH)

    loads = [
        pltpu.make_async_copy(src, dst, local.at[n])
        for n, (src, dst) in enumerate(
            [(r_hbm, r_ref), (l1_hbm, l1_ref), (l2_hbm, l2_ref), (d1_hbm, d1_ref), (d2_hbm, d2_ref)]
        )
    ]
    for copy in loads:
        copy.start()

    def remote(m, src, dst, device, arrival=None):
        return pltpu.make_async_remote_copy(
            src_ref=src,
            dst_ref=dst,
            send_sem=send.at[m],
            recv_sem=recv.at[m if arrival is None else arrival],
            device_id=device,
            device_id_type=MESH,
        )

    def push(m, src, dst, device, arrival=None):
        copy = remote(m, src, dst, device, arrival)
        copy.start()
        pending.append(copy)

    def arrive(m, dst):
        remote(m, dst, dst, sibling).wait_recv()

    s1 = seg1[q]
    s2 = seg2[q]
    parent = par2[s2]
    loads[1].wait()
    for a in range(2):
        m1 = pat1[s1, p + NB * a].astype(F32)
        g1[q, a] = (l1_ref[pl.ds(B * a, B), :] * m1).T
    mb = (pat2[s2, 2 * NB + p] * (seg1[p] == parent).astype(jnp.int32)).astype(F32)
    loads[2].wait()
    own_b = (l2_ref[pl.ds(2 * B, B), :] * mb).T
    bz[p] = own_b
    pl.semaphore_wait(barrier, len(partners))

    def prepare_root():
        loads[0].wait()
        for a in range(2):
            gr[y, a] = r_ref[pl.ds(a, 2 * B, stride=2), :].T

    def prepare_rest():
        gbd[q, 0] = own_b
        for a in range(2):
            ma = (pat2[s2, p + NB * a] * pat1[parent, p + NB * a]).astype(F32)
            ew[:, pl.ds(B * a, B)] = (l2_ref[pl.ds(B * a, B), :] * ma).T
        loads[3].wait()
        gbd[q, 1] = d1_ref[...].T
        loads[4].wait()

    def gather_root():
        for n, step in enumerate(STEPS):
            push(M_ROOT + n, gr.at[y], gr.at[y], at(0, step))
        yield
        for n, step in enumerate(STEPS):
            arrive(M_ROOT + n, gr.at[(y + NY - step) % NY])

    def gather(g, base):
        def slot(h, du, dv):
            dx, dy = (du, dv) if h == 0 else (dv, du)
            return g.at[((y + dy) % NY) * NX + (x + dx) % NX, h]

        def first(h, n):
            view = slot(h, 0, 0)
            step = STEPS[n]
            push(base + 15 * h + n, view, view, at(step, 0) if h == 0 else at(0, step))

        def second(h, i, n):
            view = slot(h, OFFSETS[i], 0)
            step = STEPS[n]
            push(base + 15 * h + 3 + 3 * i + n, view, view, at(0, step) if h == 0 else at(step, 0))

        def got_first(h, n):
            arrive(base + 15 * h + n, slot(h, 4 - STEPS[n], 0))

        def got_second(h, i, n):
            arrive(base + 15 * h + 3 + 3 * i + n, slot(h, OFFSETS[i], 4 - STEPS[n]))

        for n in range(3):
            first(0, n)
            second(1, 0, n)
        for n in range(3):
            first(1, n)
            second(0, 0, n)
        yield
        for n in range(3):
            for h in range(2):
                got_first(h, n)
                for m in range(3):
                    second(h, 1 + n, m)
        for n in range(3):
            got_second(1, 0, n)
        yield
        for n in range(3):
            got_second(0, 0, n)
        for i in range(1, 4):
            for n in range(3):
                for h in range(2):
                    got_second(h, i, n)

    def column():
        def slot(dz, core):
            return bz.at[2 * ((z + dz + NZ) % NZ) + core]

        def send_to(m, dz, device):
            view = slot(dz, c)
            push(M_BZ + m, view, view, device)

        send_to(0, 0, z_up)
        send_to(4, 0, z_down)
        send_to(7, 0, sibling)
        yield
        for t in range(1, 5):
            arrive(M_BZ + t - 1, slot(-t, c))
            if t < 4:
                send_to(t, -t, z_up)
            send_to(7 + t, -t, sibling)
            if t < 4:
                arrive(M_BZ + 4 + t - 1, slot(t, c))
                if t < 3:
                    send_to(4 + t, t, z_down)
                send_to(11 + t, t, sibling)
            yield
        arrive(M_BZ + 7, slot(0, 1 - c))
        for t in range(1, 5):
            arrive(M_BZ + 7 + t, slot(-t, 1 - c))
            if t < 4:
                arrive(M_BZ + 11 + t, slot(t, 1 - c))

    def reduce(part, other, up, down, base):
        order = (4, -3, 3, -2, 2, -1, 1, 0)

        def there(off):
            return (z + off + NZ) % NZ

        for n, off in enumerate(order):
            push(base + n, part.at[1 - c, there(off)], other.at[there(off)], sibling)
        yield

        def own(n, i):
            d = there(order[n])
            if i == 0:
                arrive(base + n, other.at[d])
            return part[c, d, i] + other[d, i]

        def hop(n, t, i, buffer, m, device):
            total = own(n, i)
            if t > 0:
                arrive(m + 2 * (t - 1) + i, buffer.at[t - 1, i])
                total = total + buffer[t - 1, i]
            d = there(order[n])
            part[c, d, i] = total
            push(m + 2 * t + i, part.at[c, d, i], buffer.at[t, i], device)

        for t in range(4):
            for i in range(2):
                hop(2 * t, t, i, up, base + 8, z_up)
                if t < 3:
                    hop(2 * t + 1, t, i, down, base + 16, z_down)
            yield
        for i in range(2):
            total = own(7, i)
            arrive(base + 20 + i, down.at[2, i])
            total = total + down[2, i]
            arrive(base + 14 + i, up.at[3, i])
            part[c, z, i] = total + up[3, i]

    def reduce_panel(part, other, chain, base):
        UP, DOWN = 0, 2
        offsets = (4 - odd, 2 - 5 * odd, 3 * odd - 2, 0 - odd)
        rows = [((z + off + NZ) % NZ) // 2 for off in offsets]
        even_sent, odd_sent = [], []
        odd_chip = jnp.logical_not(lands)

        def wait_own(n):
            arrive(base + n, other.at[rows[n]])

        def own(n, i):
            return part[c, rows[n], i] + other[rows[n], i]

        def got(kind, i):
            arrive(base + 4 + 4 * kind + i, chain.at[kind, i])
            return chain[kind, i]

        def onward(sent, n, i, kind, total):
            part[c, rows[n], i] = total
            device = z_up if kind < DOWN else z_down
            copy = remote(
                base + 4 + 4 * kind + i, part.at[c, rows[n], i], chain.at[kind, i], device
            )
            copy.start()
            sent.append((base + 4 + 4 * kind + i, rows[n], i, kind))

        for n in range(4):
            push(base + n, part.at[1 - c, rows[n]], other.at[rows[n]], sibling)
        yield

        @pl.when(lands)
        def _():
            wait_own(0)
            for i in range(2):
                onward(even_sent, 0, i, UP, own(0, i))
                onward(even_sent, 0, i + 2, DOWN, own(0, i + 2))

        @pl.when(odd_chip)
        def _():
            wait_own(0)
            wait_own(1)
            for i in range(2):
                onward(odd_sent, 0, i + 2, UP, own(0, i + 2))
                onward(odd_sent, 1, i, DOWN, own(1, i))

        yield

        @pl.when(odd_chip)
        def _():
            for i in range(2):
                onward(odd_sent, 0, i, UP, own(0, i) + got(UP, i))
                onward(odd_sent, 1, i + 2, DOWN, own(1, i + 2) + got(DOWN, i + 2))

        @pl.when(lands)
        def _():
            wait_own(1)
            wait_own(2)
            for i in range(2):
                onward(even_sent, 1, i + 2, UP + 1, own(1, i + 2) + got(UP, i + 2))
                onward(even_sent, 2, i, DOWN + 1, own(2, i) + got(DOWN, i))

        yield

        @pl.when(odd_chip)
        def _():
            wait_own(2)
            wait_own(3)
            for i in range(2):
                onward(odd_sent, 2, i + 2, UP + 1, own(2, i + 2) + got(UP + 1, i + 2))
                onward(odd_sent, 3, i, DOWN + 1, own(3, i) + got(DOWN + 1, i))

        @pl.when(lands)
        def _():
            for i in range(2):
                onward(even_sent, 1, i, UP + 1, own(1, i) + got(UP, i))
                onward(even_sent, 2, i + 2, DOWN + 1, own(2, i + 2) + got(DOWN, i + 2))

        yield

        @pl.when(odd_chip)
        def _():
            for i in range(2):
                onward(odd_sent, 2, i, UP + 1, own(2, i) + got(UP + 1, i))
                onward(odd_sent, 3, i + 2, DOWN + 1, own(3, i + 2) + got(DOWN + 1, i + 2))

        yield

        @pl.when(lands)
        def _():
            wait_own(3)
            for i in range(4):
                part[c, rows[3], i] = own(3, i) + got(UP + 1, i) + got(DOWN + 1, i)

        def drain():
            for condition, sent in ((lands, even_sent), (odd_chip, odd_sent)):
                @pl.when(condition)
                def _():
                    for m, row, i, kind in sent:
                        remote(m, part.at[c, row, i], chain.at[kind, i], z_up).wait_send()

        drains.append(drain)

    core = x % 2
    keeps = lands & (c == core)

    def hand_over(part, yt, base):
        for step in (1, 3, 2):
            @pl.when(lands)
            def _():
                i = (x + step) % NX
                remote(
                    base + step, part.at[c, z // 2, i], yt.at[c], (2 * z + core, y * NX + i), base + c
                ).start()

        @pl.when(keeps)
        def _():
            yt[c] = part[c, z // 2, x]

        @pl.when(lands & (c != core))
        def _():
            remote(base, part.at[c, z // 2, x], yt.at[c], sibling, base + c).start()

    def handed_over(part, yt, base):
        @pl.when(lands)
        def _():
            for step in (1, 3, 2):
                i = (x + step) % NX
                remote(
                    base + step, part.at[c, z // 2, i], yt.at[c], (2 * z + core, y * NX + i), base + c
                ).wait_send()

        @pl.when(lands & (c != core))
        def _():
            remote(base, part.at[c, z // 2, x], yt.at[c], sibling, base + c).wait_send()

    def take(yt, base):
        arrive(base + 1 - c, yt.at[1 - c])

        @pl.when(jnp.logical_not(keeps))
        def _():
            arrive(base + c, yt.at[c])

        return right3(yt[...].reshape(2 * B, B))

    GROUP = 4

    def panel(g, i):
        rows = pl.ds(i * GROUP, GROUP)
        return jnp.concatenate(
            [g[rows, 0].reshape(GROUP * B, B), g[rows, 1].reshape(GROUP * B, B)], axis=1
        )

    def times_root(g, part):
        right = right3(
            jnp.concatenate(
                [
                    jnp.concatenate([g[y * NX + i, 0].T, g[y * NX + i, 1].T], axis=0)
                    for i in range(NX)
                ],
                axis=1,
            )
        )
        for a in range(2):
            out = dot(left3(gr[:, a].reshape(NY * B, 2 * B)), right)
            for i in range(NX):
                part[a, :, i] = out[:, B * i : B * i + B].reshape(NY, B, B)

    def store_halves(part, i, out):
        rows = pl.ds(i * 2, 2)
        blocks = out.reshape(2, 2, B, B)
        part[0, rows] = blocks[:, :, : B // 2]
        part[1, rows] = blocks[:, :, B // 2 :]

    def finish(part, w, base):
        push(base, part.at[c, z, 1 - c], w.at[c], sibling)
        w[c] = part[c, z, c]
        arrive(base, w.at[1 - c])

    first, bcol, root = gather(g1, M_G1), column(), gather_root()
    whole, bd = gather(ge, M_GE), gather(gbd, M_BD)
    next(first)
    next(bcol)
    prepare_root()
    prepare_rest()
    next(first)
    next(root)
    rounds(bcol, first)
    next(bd)

    @pl.loop(0, NB)
    def _(k):
        right = right3(jnp.concatenate([g1[k, 0], g1[k, 1]], axis=1))
        ew[...] -= dot(left3(bz[k]), right)

    ge[q, 0] = ew[:, :B]
    ge[q, 1] = ew[:, B:]
    next(whole)
    rounds(root)
    times_root(g1, p1)

    def first_level():
        yield from reduce_panel(p1, x1, ch1, M_Y1)
        hand_over(p1, yt1, M_T1)
        yield
        right = take(yt1, M_T1)

        @pl.loop(0, NB // GROUP)
        def _(i):
            store_halves(pz1, i, dot(left3(panel(g1, i)), right))

        yield from reduce(pz1, xz1, upz1, dnz1, M_Z1)

    def second_level():
        yield from reduce_panel(p2, x2, ch2, M_Y2)
        hand_over(p2, yt2, M_T2)

    level_one, level_two = first_level(), second_level()
    next(level_one)
    next(level_one)
    next(whole)
    next(bd)
    times_root(ge, p2)
    next(level_two)
    until(level_two, level_one)
    rounds(bd, whole)

    def corner_step(k, acc):
        return acc + dot(left3(bz[k]), right3(gbd[k, 1]))

    u3 = right3(lax.fori_loop(0, NB, corner_step, jnp.zeros((B, B), F32)).T)
    y3 = take(yt2, M_T2)

    @pl.loop(0, NB // GROUP)
    def _(i):
        out = dot(left3(panel(ge, i)), y3)
        out = out + dot(left3(gbd[pl.ds(i * GROUP, GROUP), 0].reshape(GROUP * B, B)), u3)
        store_halves(pz2, i, out)

    rounds(reduce(pz2, xz2, upz2, dnz2, M_Z2), level_one)

    finish(pz1, w1, M_F1)
    finish(pz2, w2, M_F2)
    same1 = (seg1[p] == seg1[q]).astype(F32)
    same2 = (seg2[p] == seg2[q]).astype(F32)
    o1_ref[...] = (d1_ref[...] + w1[...].reshape(B, B)) * same1
    o2_ref[...] = (d2_ref[...] + w2[...].reshape(B, B)) * same2

    for copy in pending:
        copy.wait_send()
    for drain in drains:
        drain()
    handed_over(p1, yt1, M_T1)
    handed_over(p2, yt2, M_T2)


def on_device(
    root_inverse, lower_one, lower_two, dinv_one, dinv_two,
    seg_one, seg_two, parent_two, pattern_one, pattern_two,
):
    vmem = pl.BlockSpec(memory_space=pltpu.VMEM)
    smem = pl.BlockSpec(memory_space=pltpu.SMEM)
    hbm = pl.BlockSpec(memory_space=pltpu.HBM)

    def buf(*shape):
        return pltpu.VMEM(shape, F32)

    panel_sum = [buf(2, NY, NX, B, B), buf(NY, NX, B, B), buf(4, NX, B, B)]
    half = B // 2
    block_sum = [
        buf(2, NZ, 2, half, B),
        buf(NZ, 2, half, B),
        buf(4, 2, half, B),
        buf(3, 2, half, B),
    ]

    outs = pl.pallas_call(
        kernel,
        out_shape=[jax.ShapeDtypeStruct((B, B), F32)] * 2,
        in_specs=[smem] * 5 + [hbm] * 5,
        out_specs=[vmem] * 2,
        scratch_shapes=[
            buf(4 * B, B),
            buf(2 * B, B),
            buf(3 * B, B),
            buf(B, B),
            buf(B, B),
            buf(NY, 2, B, 2 * B),
            buf(NB, 2, B, B),
            buf(NB, 2, B, B),
            buf(NB, 2, B, B),
            buf(NB, B, B),
            *panel_sum,
            *panel_sum,
            *block_sum,
            *block_sum,
            buf(2, B, B),
            buf(2, B, B),
            buf(2, B // 2, B),
            buf(2, B // 2, B),
            buf(B, 2 * B),
            pltpu.SemaphoreType.DMA((M_ALL,)),
            pltpu.SemaphoreType.DMA((M_ALL,)),
            pltpu.SemaphoreType.DMA((5,)),
        ],
        compiler_params=pltpu.CompilerParams(
            collective_id=0, has_side_effects=True, vmem_limit_bytes=56 << 20
        ),
    )(
        seg_one, seg_two, parent_two, pattern_one, pattern_two,
        root_inverse.reshape(4 * B, B),
        lower_one.reshape(2 * B, B),
        lower_two.reshape(3 * B, B),
        dinv_one.reshape(B, B),
        dinv_two.reshape(B, B),
    )
    return tuple(out.reshape(1, 1, B, 1, 1, B) for out in outs)


def solution(mesh):
    blocks = P(None, "prow", None, None, "pcol", None)
    return jax.shard_map(
        on_device,
        mesh=mesh,
        in_specs=(blocks,) * 5 + (P(),) * 5,
        out_specs=(blocks,) * 2,
        check_vma=False,
    )
```

time: 132 us -> 107 us (0.81)
  Pallas kernels: 124 us -> 105 us
  local copies, waits for them, and re-layouts: 6.4 us -> 2.14 us
    pallas_call x1, Pallas kernels: 124 us -> 105 us  [on_device(): pl.pallas_call(kernel, out_shape=[jax.ShapeDtypeStruct((B, B), F32)] * 2,...]
    unnamed x22 -> x4, local copies, waits for them, and re-layouts: 6.4 us -> 2.14 us
where the time goes in v2:
time: 107 us
  Pallas kernels  105 us (98%)
  local copies, waits for them, and re-layouts  2.14 us (2%)
    pallas_call x1, Pallas kernels, on_device(): pl.pallas_call(kernel, out_shape=[jax.ShapeDtypeStruct((B, B), F32)] * 2,...  105 us

profile of v2, /device:TPU:1, one launch (start us, length us, event | category | flops | bytes accessed | tf_op | source)
XLA Modules:
  0.0 107.3 jit_solution(13958350938592063468)
XLA Ops:
  0.6 104.5 %shard_map.113 = (f32[128,128]{1,0:T(8,128)}, f32[128,128]{1,0:T(8,128)}) custom-call(s32[16]{0:T(128)} %seg1.1, s32[16]{0:T(128)} %seg2.1, s32[4]{0:T(128)} %par2.1, s32[3,32]{1,0:T(4,128)} %pat1.1, s32[4,48]{1,0:T(4,128)} %pat2.1, f32[512,128]{1,0:T(8,128)} %bitcast.11, f32[256,128]{1,0:T(8,128)} %bitcast.13, f32[384,128]{1,0:T(8,128)} %bitcast.12, ...), custom_call_target="tpu_custom_call" | custom-call | tf_op jit(solution)/shard_map/pallas_call | solution.py:556
  105.2 0.0 copy-start
  105.2 1.5 %copy.16 = f32[1,1,128,1,1,128]{5,4,3,2,1,0:T(1,128)} copy(f32[1,1,128,1,1,128]{5,4,3,2,1,0:T(1,128)} %bitcast.17) | data formatting | bytes 131072
  106.7 0.0 copy-done
  106.7 0.6 copy.17
Async XLA Ops:
  105.2 1.5 %copy-start = (f32[128,128]{1,0:T(8,128)S(1)}, f32[128,128]{1,0:T(8,128)}, u32[]{:S(2)}) copy-start(f32[128,128]{1,0:T(8,128)} %get-tuple-element.5) | copy-start | bytes 196612

commit v3 on v2

--- a/solution.py
+++ b/solution.py
@@ -50,14 +50,6 @@
 
 def dot(a, b):
     return jnp.dot(a, b, preferred_element_type=F32)
-
-
-def until(flow, *others):
-    others = list(others)
-    for _ in flow:
-        for other in list(others):
-            if next(other, "end") == "end":
-                others.remove(other)
 
 
 def rounds(*flows):
@@ -102,7 +94,7 @@
 
     barrier = pltpu.get_barrier_semaphore()
     partners = [at(1, 0), at(2, 0), at(3, 0), at(0, 1), at(0, 2), at(0, 3)]
-    partners += [sibling, z_up, z_down]
+    partners += [sibling] + [(2 * ((z + d) % NZ) + c, q) for d in range(1, NZ)]
     partners += [(2 * z + 1 - c, y * NX + (x + d) % NX) for d in (1, 2, 3)]
     for device in partners:
         pl.semaphore_signal(barrier, inc=1, device_id=device, device_id_type=MESH)
@@ -140,7 +132,7 @@
     loads[1].wait()
     for a in range(2):
         m1 = pat1[s1, p + NB * a].astype(F32)
-        g1[q, a] = (l1_ref[pl.ds(B * a, B), :] * m1).T
+        g1[q, pl.ds(B * a, B)] = (l1_ref[pl.ds(B * a, B), :] * m1).T
     mb = (pat2[s2, 2 * NB + p] * (seg1[p] == parent).astype(jnp.int32)).astype(F32)
     loads[2].wait()
     own_b = (l2_ref[pl.ds(2 * B, B), :] * mb).T
@@ -153,12 +145,12 @@
             gr[y, a] = r_ref[pl.ds(a, 2 * B, stride=2), :].T
 
     def prepare_rest():
-        gbd[q, 0] = own_b
+        gbd[q, :B] = own_b
         for a in range(2):
             ma = (pat2[s2, p + NB * a] * pat1[parent, p + NB * a]).astype(F32)
             ew[:, pl.ds(B * a, B)] = (l2_ref[pl.ds(B * a, B), :] * ma).T
         loads[3].wait()
-        gbd[q, 1] = d1_ref[...].T
+        gbd[q, B:] = d1_ref[...].T
         loads[4].wait()
 
     def gather_root():
@@ -168,10 +160,11 @@
         for n, step in enumerate(STEPS):
             arrive(M_ROOT + n, gr.at[(y + NY - step) % NY])
 
-    def gather(g, base):
+    def gather(g, base, cut=B):
         def slot(h, du, dv):
             dx, dy = (du, dv) if h == 0 else (dv, du)
-            return g.at[((y + dy) % NY) * NX + (x + dx) % NX, h]
+            rows = pl.ds(0, cut) if h == 0 else pl.ds(cut, 2 * B - cut)
+            return g.at[((y + dy) % NY) * NX + (x + dx) % NX, rows]
 
         def first(h, n):
             view = slot(h, 0, 0)
@@ -212,33 +205,23 @@
                     got_second(h, i, n)
 
     def column():
-        def slot(dz, core):
-            return bz.at[2 * ((z + dz + NZ) % NZ) + core]
-
-        def send_to(m, dz, device):
-            view = slot(dz, c)
-            push(M_BZ + m, view, view, device)
-
-        send_to(0, 0, z_up)
-        send_to(4, 0, z_down)
-        send_to(7, 0, sibling)
-        yield
-        for t in range(1, 5):
-            arrive(M_BZ + t - 1, slot(-t, c))
-            if t < 4:
-                send_to(t, -t, z_up)
-            send_to(7 + t, -t, sibling)
-            if t < 4:
-                arrive(M_BZ + 4 + t - 1, slot(t, c))
-                if t < 3:
-                    send_to(4 + t, t, z_down)
-                send_to(11 + t, t, sibling)
-            yield
+        turns = (1, 7, 2, 6, 3, 5, 4)
+
+        def slot(turn, core):
+            return bz.at[2 * ((z + turn) % NZ) + core]
+
+        for n, turn in enumerate(turns):
+            device = (2 * ((z + turn) % NZ) + c, q)
+            push(M_BZ + n, slot(0, c), slot(0, c), device)
+        push(M_BZ + 7, slot(0, c), slot(0, c), sibling)
+        yield
+        for n, turn in enumerate(turns):
+            arrive(M_BZ + n, slot(NZ - turn, c))
+            push(M_BZ + 8 + n, slot(NZ - turn, c), slot(NZ - turn, c), sibling)
+        yield
         arrive(M_BZ + 7, slot(0, 1 - c))
-        for t in range(1, 5):
-            arrive(M_BZ + 7 + t, slot(-t, 1 - c))
-            if t < 4:
-                arrive(M_BZ + 11 + t, slot(t, 1 - c))
+        for n, turn in enumerate(turns):
+            arrive(M_BZ + 8 + n, slot(NZ - turn, 1 - c))
 
     def reduce(part, other, up, down, base):
         order = (4, -3, 3, -2, 2, -1, 1, 0)
@@ -427,14 +410,14 @@
     def panel(g, i):
         rows = pl.ds(i * GROUP, GROUP)
         return jnp.concatenate(
-            [g[rows, 0].reshape(GROUP * B, B), g[rows, 1].reshape(GROUP * B, B)], axis=1
+            [g[rows, :B].reshape(GROUP * B, B), g[rows, B:].reshape(GROUP * B, B)], axis=1
         )
 
     def times_root(g, part):
         right = right3(
             jnp.concatenate(
                 [
-                    jnp.concatenate([g[y * NX + i, 0].T, g[y * NX + i, 1].T], axis=0)
+                    jnp.concatenate([g[y * NX + i, :B].T, g[y * NX + i, B:].T], axis=0)
                     for i in range(NX)
                 ],
                 axis=1,
@@ -456,24 +439,25 @@
         w[c] = part[c, z, c]
         arrive(base, w.at[1 - c])
 
-    first, bcol, root = gather(g1, M_G1), column(), gather_root()
+    first, bcol, root = gather(g1, M_G1, 64), column(), gather_root()
     whole, bd = gather(ge, M_GE), gather(gbd, M_BD)
     next(first)
     next(bcol)
     prepare_root()
-    prepare_rest()
     next(first)
     next(root)
-    rounds(bcol, first)
+    prepare_rest()
+    next(bcol)
+    rounds(first, bcol)
     next(bd)
 
-    @pl.loop(0, NB)
-    def _(k):
-        right = right3(jnp.concatenate([g1[k, 0], g1[k, 1]], axis=1))
-        ew[...] -= dot(left3(bz[k]), right)
-
-    ge[q, 0] = ew[:, :B]
-    ge[q, 1] = ew[:, B:]
+    @pl.loop(0, NB // GROUP)
+    def _(i):
+        left = jnp.concatenate([bz[i * GROUP + k] for k in range(GROUP)], axis=1)
+        ew[...] -= dot(left3(left), right3(panel(g1, i)))
+
+    ge[q, :B] = ew[:, :B]
+    ge[q, B:] = ew[:, B:]
     next(whole)
     rounds(root)
     times_root(g1, p1)
@@ -481,42 +465,44 @@
     def first_level():
         yield from reduce_panel(p1, x1, ch1, M_Y1)
         hand_over(p1, yt1, M_T1)
-        yield
-        right = take(yt1, M_T1)
-
-        @pl.loop(0, NB // GROUP)
-        def _(i):
-            store_halves(pz1, i, dot(left3(panel(g1, i)), right))
-
-        yield from reduce(pz1, xz1, upz1, dnz1, M_Z1)
 
     def second_level():
         yield from reduce_panel(p2, x2, ch2, M_Y2)
         hand_over(p2, yt2, M_T2)
 
     level_one, level_two = first_level(), second_level()
+    next(level_one)
     next(level_one)
     next(level_one)
     next(whole)
     next(bd)
     times_root(ge, p2)
     next(level_two)
-    until(level_two, level_one)
+    next(level_two)
+    rounds(level_one, level_two)
     rounds(bd, whole)
 
     def corner_step(k, acc):
-        return acc + dot(left3(bz[k]), right3(gbd[k, 1]))
+        return acc + dot(left3(bz[k]), right3(gbd[k, B:]))
 
     u3 = right3(lax.fori_loop(0, NB, corner_step, jnp.zeros((B, B), F32)).T)
+    y1 = take(yt1, M_T1)
+
+    @pl.loop(0, NB // GROUP)
+    def _(i):
+        store_halves(pz1, i, dot(left3(panel(g1, i)), y1))
+
+    last_one = reduce(pz1, xz1, upz1, dnz1, M_Z1)
+    next(last_one)
     y3 = take(yt2, M_T2)
 
     @pl.loop(0, NB // GROUP)
     def _(i):
         out = dot(left3(panel(ge, i)), y3)
-        out = out + dot(left3(gbd[pl.ds(i * GROUP, GROUP), 0].reshape(GROUP * B, B)), u3)
+        out = out + dot(left3(gbd[pl.ds(i * GROUP, GROUP), :B].reshape(GROUP * B, B)), u3)
         store_halves(pz2, i, out)
 
-    rounds(reduce(pz2, xz2, upz2, dnz2, M_Z2), level_one)
+    rounds(reduce(pz2, xz2, upz2, dnz2, M_Z2), last_one)
 
     finish(pz1, w1, M_F1)
     finish(pz2, w2, M_F2)
@@ -565,9 +551,9 @@
             buf(B, B),
             buf(B, B),
             buf(NY, 2, B, 2 * B),
-            buf(NB, 2, B, B),
-            buf(NB, 2, B, B),
-            buf(NB, 2, B, B),
+            buf(NB, 2 * B, B),
+            buf(NB, 2 * B, B),
+            buf(NB, 2 * B, B),
             buf(NB, B, B),
             *panel_sum,
             *panel_sum,

time: 107 us -> 97.6 us (0.912)
  Pallas kernels: 105 us -> 94.6 us
    pallas_call x1, Pallas kernels: 105 us -> 94.6 us  [on_device(): pl.pallas_call(kernel, out_shape=[jax.ShapeDtypeStruct((B, B), F32)] * 2,...]
where the time goes in v3:
time: 97.6 us; the launch traced here: 97.4 us
  Pallas kernels  94.6 us (97%)
  local copies, waits for them, and re-layouts  2.14 us (2%)
    pallas_call x1, Pallas kernels, on_device(): pl.pallas_call(kernel, out_shape=[jax.ShapeDtypeStruct((B, B), F32)] * 2,...  94.6 us
    unnamed x4, local copies, waits for them, and re-layouts  2.14 us

profile of v3, /device:TPU:1, one launch (start us, length us, event | category | flops | bytes accessed | tf_op | source)
XLA Modules:
  0.0 97.4 jit_solution(9973957441553414492)
XLA Ops:
  0.6 94.6 %shard_map.113 = (f32[128,128]{1,0:T(8,128)}, f32[128,128]{1,0:T(8,128)}) custom-call(s32[16]{0:T(128)} %seg1.1, s32[16]{0:T(128)} %seg2.1, s32[4]{0:T(128)} %par2.1, s32[3,32]{1,0:T(4,128)} %pat1.1, s32[4,48]{1,0:T(4,128)} %pat2.1, f32[512,128]{1,0:T(8,128)} %bitcast.11, f32[256,128]{1,0:T(8,128)} %bitcast.13, f32[384,128]{1,0:T(8,128)} %bitcast.12, ...), custom_call_target="tpu_custom_call" | custom-call | tf_op jit(solution)/shard_map/pallas_call | solution.py:542
  95.2 0.0 copy-start
  95.3 1.5 %copy.16 = f32[1,1,128,1,1,128]{5,4,3,2,1,0:T(1,128)} copy(f32[1,1,128,1,1,128]{5,4,3,2,1,0:T(1,128)} %bitcast.17) | data formatting | bytes 131072
  96.8 0.0 copy-done
  96.8 0.6 copy.17
Async XLA Ops:
  95.2 1.5 %copy-start = (f32[128,128]{1,0:T(8,128)S(1)}, f32[128,128]{1,0:T(8,128)}, u32[]{:S(2)}) copy-start(f32[128,128]{1,0:T(8,128)} %get-tuple-element.5) | copy-start | bytes 196612

commit v4 on v3

--- a/solution.py
+++ b/solution.py
@@ -52,7 +52,7 @@
     return jnp.dot(a, b, preferred_element_type=F32)
 
 
-def rounds(*flows):
+def rounds(*flows, between=None):
     flows = list(flows)
     while flows:
         for flow in list(flows):
@@ -60,6 +60,8 @@
                 next(flow)
             except StopIteration:
                 flows.remove(flow)
+        if between is not None:
+            between()
 
 
 def kernel(
@@ -123,6 +125,11 @@
         copy.start()
         pending.append(copy)
 
+    def settle(count):
+        for copy in pending[:count]:
+            copy.wait_send()
+        del pending[:count]
+
     def arrive(m, dst):
         remote(m, dst, dst, sibling).wait_recv()
 
@@ -261,7 +268,7 @@
             arrive(base + 14 + i, up.at[3, i])
             part[c, z, i] = total + up[3, i]
 
-    def reduce_panel(part, other, chain, base):
+    def reduce_panel(part, other, chain, base, product):
         UP, DOWN = 0, 2
         offsets = (4 - odd, 2 - 5 * odd, 3 * odd - 2, 0 - odd)
         rows = [((z + off + NZ) % NZ) // 2 for off in offsets]
@@ -287,8 +294,10 @@
             copy.start()
             sent.append((base + 4 + 4 * kind + i, rows[n], i, kind))
 
+        product(1 - c)
         for n in range(4):
             push(base + n, part.at[1 - c, rows[n]], other.at[rows[n]], sibling)
+        product(c)
         yield
 
         @pl.when(lands)
@@ -423,10 +432,13 @@
                 axis=1,
             )
         )
-        for a in range(2):
+
+        def product(a):
             out = dot(left3(gr[:, a].reshape(NY * B, 2 * B)), right)
             for i in range(NX):
                 part[a, :, i] = out[:, B * i : B * i + B].reshape(NY, B, B)
+
+        return product
 
     def store_halves(part, i, out):
         rows = pl.ds(i * 2, 2)
@@ -448,8 +460,8 @@
     next(root)
     prepare_rest()
     next(bcol)
+    next(bd)
     rounds(first, bcol)
-    next(bd)
 
     @pl.loop(0, NB // GROUP)
     def _(i):
@@ -460,14 +472,13 @@
     ge[q, B:] = ew[:, B:]
     next(whole)
     rounds(root)
-    times_root(g1, p1)
 
     def first_level():
-        yield from reduce_panel(p1, x1, ch1, M_Y1)
+        yield from reduce_panel(p1, x1, ch1, M_Y1, times_root(g1, p1))
         hand_over(p1, yt1, M_T1)
 
     def second_level():
-        yield from reduce_panel(p2, x2, ch2, M_Y2)
+        yield from reduce_panel(p2, x2, ch2, M_Y2, times_root(ge, p2))
         hand_over(p2, yt2, M_T2)
 
     level_one, level_two = first_level(), second_level()
@@ -476,10 +487,9 @@
     next(level_one)
     next(whole)
     next(bd)
-    times_root(ge, p2)
     next(level_two)
     next(level_two)
-    rounds(level_one, level_two)
+    rounds(level_one, level_two, between=lambda: settle(8))
     rounds(bd, whole)
 
     def corner_step(k, acc):
@@ -502,7 +512,7 @@
         out = out + dot(left3(gbd[pl.ds(i * GROUP, GROUP), :B].reshape(GROUP * B, B)), u3)
         store_halves(pz2, i, out)
 
-    rounds(reduce(pz2, xz2, upz2, dnz2, M_Z2), last_one)
+    rounds(reduce(pz2, xz2, upz2, dnz2, M_Z2), last_one, between=lambda: settle(16))
 
     finish(pz1, w1, M_F1)
     finish(pz2, w2, M_F2)

time: 97.6 us -> 98.1 us (level)
  no operation moved by 1% of the time
where the time goes in v4:
time: 98.1 us; the launch traced here: 97.9 us
  Pallas kernels  95.1 us (97%)
  local copies, waits for them, and re-layouts  2.14 us (2%)
    pallas_call x1, Pallas kernels, on_device(): pl.pallas_call(kernel, out_shape=[jax.ShapeDtypeStruct((B, B), F32)] * 2,...  95.1 us
    unnamed x4, local copies, waits for them, and re-layouts  2.14 us

profile of v4, /device:TPU:1, one launch (start us, length us, event | category | flops | bytes accessed | tf_op | source)
XLA Modules:
  0.0 97.9 jit_solution(2578197752607376522)
XLA Ops:
  0.6 95.1 %shard_map.113 = (f32[128,128]{1,0:T(8,128)}, f32[128,128]{1,0:T(8,128)}) custom-call(s32[16]{0:T(128)} %seg1.1, s32[16]{0:T(128)} %seg2.1, s32[4]{0:T(128)} %par2.1, s32[3,32]{1,0:T(4,128)} %pat1.1, s32[4,48]{1,0:T(4,128)} %pat2.1, f32[512,128]{1,0:T(8,128)} %bitcast.11, f32[256,128]{1,0:T(8,128)} %bitcast.13, f32[384,128]{1,0:T(8,128)} %bitcast.12, ...), custom_call_target="tpu_custom_call" | custom-call | tf_op jit(solution)/shard_map/pallas_call | solution.py:552
  95.8 0.0 copy-start
  95.8 1.5 %copy.16 = f32[1,1,128,1,1,128]{5,4,3,2,1,0:T(1,128)} copy(f32[1,1,128,1,1,128]{5,4,3,2,1,0:T(1,128)} %bitcast.17) | data formatting | bytes 131072
  97.3 0.0 copy-done
  97.3 0.6 copy.17
Async XLA Ops:
  95.8 1.5 %copy-start = (f32[128,128]{1,0:T(8,128)S(1)}, f32[128,128]{1,0:T(8,128)}, u32[]{:S(2)}) copy-start(f32[128,128]{1,0:T(8,128)} %get-tuple-element.5) | copy-start | bytes 196612

commit v5 on v3

--- a/solution.py
+++ b/solution.py
@@ -437,7 +437,6 @@
     def finish(part, w, base):
         push(base, part.at[c, z, 1 - c], w.at[c], sibling)
         w[c] = part[c, z, c]
-        arrive(base, w.at[1 - c])
 
     first, bcol, root = gather(g1, M_G1, 64), column(), gather_root()
     whole, bd = gather(ge, M_GE), gather(gbd, M_BD)
@@ -506,6 +505,8 @@
 
     finish(pz1, w1, M_F1)
     finish(pz2, w2, M_F2)
+    arrive(M_F1, w1.at[1 - c])
+    arrive(M_F2, w2.at[1 - c])
     same1 = (seg1[p] == seg1[q]).astype(F32)
     same2 = (seg2[p] == seg2[q]).astype(F32)
     o1_ref[...] = (d1_ref[...] + w1[...].reshape(B, B)) * same1

time: 97.6 us -> 97 us (level)
  no operation moved by 1% of the time
where the time goes in v5:
time: 97 us; the launch traced here: 96.9 us
  Pallas kernels  94.1 us (97%)
  local copies, waits for them, and re-layouts  2.14 us (2%)
    pallas_call x1, Pallas kernels, on_device(): pl.pallas_call(kernel, out_shape=[jax.ShapeDtypeStruct((B, B), F32)] * 2,...  94.1 us
    unnamed x4, local copies, waits for them, and re-layouts  2.14 us

profile of v5, /device:TPU:1, one launch (start us, length us, event | category | flops | bytes accessed | tf_op | source)
XLA Modules:
  0.0 96.9 jit_solution(15179468542787777474)
XLA Ops:
  0.6 94.1 %shard_map.113 = (f32[128,128]{1,0:T(8,128)}, f32[128,128]{1,0:T(8,128)}) custom-call(s32[16]{0:T(128)} %seg1.1, s32[16]{0:T(128)} %seg2.1, s32[4]{0:T(128)} %par2.1, s32[3,32]{1,0:T(4,128)} %pat1.1, s32[4,48]{1,0:T(4,128)} %pat2.1, f32[512,128]{1,0:T(8,128)} %bitcast.11, f32[256,128]{1,0:T(8,128)} %bitcast.13, f32[384,128]{1,0:T(8,128)} %bitcast.12, ...), custom_call_target="tpu_custom_call" | custom-call | tf_op jit(solution)/shard_map/pallas_call | solution.py:543
  94.7 0.0 copy-start
  94.7 1.5 %copy.16 = f32[1,1,128,1,1,128]{5,4,3,2,1,0:T(1,128)} copy(f32[1,1,128,1,1,128]{5,4,3,2,1,0:T(1,128)} %bitcast.17) | data formatting | bytes 131072
  96.2 0.0 copy-done
  96.2 0.6 copy.17
Async XLA Ops:
  94.7 1.5 %copy-start = (f32[128,128]{1,0:T(8,128)S(1)}, f32[128,128]{1,0:T(8,128)}, u32[]{:S(2)}) copy-start(f32[128,128]{1,0:T(8,128)} %get-tuple-element.5) | copy-start | bytes 196612
